TPU v7x, 256 devices: a whole 4x4x8 slice. The times are simulated.
256 devices in a mesh: row: 16 (over y_lo, z), col: 16 (over y_hi, x, core).
Axes of the slice: x: 4, y: 4 (y_hi: 2, y_lo: 2; y = y_hi * 2 + y_lo), z: 8, core: 2. Of those that a mesh axis runs over, the one named last changes fastest.
Arguments:
- spectra: bfloat16 [2, 2, 10240, 256], P(None, None, ('row', 'col')), may hold values from -40 to 40
- delays_s: int32 [10240, 512], P('row'), may hold values from 0 to 1023
- delays_r: int32 [10240, 512], P('col'), may hold values from 0 to 1023
- wl_index: int32 [2], replicated, may hold values from 0 to 10239
Outputs:
- beam_field: float32 [2, 2, 512, 512], P(None, None, 'col', 'row')
All inputs are finite; a program needn't handle non-finite values.
Results may differ from a plain program's by a relative error of at most 0.0071.
Values may be sent and summed in bfloat16 or wider, within the bound.
A program may use at most 64 MiB of HBM per device.

v0:
```python
import functools
import math

import jax
import jax.numpy as jnp
from jax import lax
from jax.experimental import pallas as pl
from jax.experimental.pallas import tpu as pltpu
from jax.sharding import PartitionSpec as P

MESH = pl.DeviceIdType.MESH
F32 = jnp.float32
BF16 = jnp.bfloat16

STATIONS = 10240
WINDOWS = 256
SIDE = 16
OWN = 40
SLOT = 48
HALF = 256
BEAMS = 32
RATES = (0.0361, 0.0596)

COS = (0.9999992215668542, -19.7389825153523, 64.92872658489378, -85.27239662504564, 58.79403695210448, -21.076779298561963)
SIN = (6.283182818541802, -41.34142139793358, 81.59618385577838, -76.58010036540968, 41.20539421297601, -12.271261390344423)

PW_ROW, PW_COL, X_ROW, X_COL, LV_COL, SUM_U, SUM_V, ALL_U, ALL_V = range(9)


def horner(coefs, z):
    acc = jnp.full_like(z, coefs[-1])
    for c in coefs[-2::-1]:
        acc = acc * z + c
    return acc


def kernel(
    spec_hbm, ds_hbm, dr_hbm, wl, out,
    xin, dbuf, tab, pk, xr, pw_send, pw, lv_send, lv, sums, part, block, gathered,
    load, send, recv,
):
    r, c = lax.axis_index("row"), lax.axis_index("col")
    slots = (c // 2, r // 2)
    halves = (c % 2, r % 2)
    holder = (r // 8 == halves[0], c // 8 == halves[1])
    place = (c, r)
    rank = (r, c)

    def peer(axis, other):
        return (r, other) if axis == 0 else (other, c)

    def copy(src, dst, group, s, t, device):
        return pltpu.make_async_remote_copy(
            src_ref=src, dst_ref=dst, send_sem=send.at[group, s], recv_sem=recv.at[group, t],
            device_id=device, device_id_type=MESH,
        )

    def over_peers(axis, action):
        def step(o, carry):
            action(lax.rem(place[axis] + o, SIDE))
            return carry

        lax.fori_loop(1, SIDE, step, 0)

    def load_delays(hbm, which):
        start = pl.multiple_of(halves[which] * HALF, HALF)
        return pltpu.make_async_copy(hbm.at[:, pl.ds(start, HALF)], dbuf.at[which], load.at[which])

    loads = [load_delays(ds_hbm, 0), load_delays(dr_hbm, 1)]
    load_x = pltpu.make_async_copy(spec_hbm, xin, load.at[2])
    load_x.start()
    for item in loads:
        item.start()
    barrier = pltpu.get_barrier_semaphore()
    for axis in (0, 1):
        over_peers(axis, lambda p: pl.semaphore_signal(barrier, inc=1, device_id=peer(axis, p), device_id_type=MESH))

    load_x.wait()
    lane = lax.broadcasted_iota(jnp.int32, (OWN, 128), 1)
    low = lane < 64
    column = jnp.zeros((OWN, 128), F32)
    for f in range(2):
        tiles = [[xin[f, p, :, 128 * t : 128 * t + 128].astype(F32) for t in range(2)] for p in range(2)]
        total = sum(tiles[p][t] * tiles[p][t] for p in range(2) for t in range(2))
        column = jnp.where(lane == f, jnp.sum(total, axis=1, keepdims=True), column)
        for t in range(2):
            re, im = tiles[0][t], tiles[1][t]
            first = jnp.where(low, re, pltpu.roll(im, 64, 1))
            second = jnp.where(low, pltpu.roll(re, 64, 1), im)
            for k, value in ((2 * t, first), (2 * t + 1, second)):
                pk[4 * f + k] = jnp.concatenate([value, jnp.zeros((SLOT - OWN, 128), F32)], axis=0).astype(BF16)
    rows = jnp.concatenate([column, jnp.zeros((128 - OWN, 128), F32)], axis=0).T[:8]
    station = (r * SIDE + c) * OWN + lax.broadcasted_iota(jnp.int32, (8, 128), 1)
    sub = lax.broadcasted_iota(jnp.int32, (8, 128), 0)
    inside = lax.broadcasted_iota(jnp.int32, (8, 128), 1) < OWN
    wanted = jnp.where(sub == 0, wl[0], wl[1])
    picked = jnp.sum(jnp.where(inside & (station == wanted) & (sub < 2), rows, 0.0), axis=1, keepdims=True)
    tile = jnp.where(sub < 2, rows, pltpu.roll(jnp.broadcast_to(picked, (8, 128)), 2, 0))
    pw_send[...] = tile

    pl.semaphore_wait(barrier, 2 * (SIDE - 1))

    for axis, group in ((0, PW_ROW), (1, PW_COL)):
        over_peers(axis, lambda p: copy(pw_send, pw.at[axis, place[axis]], group, p, place[axis], peer(axis, p)).start())
        pw[axis, place[axis]] = tile
    for axis, group in ((0, X_ROW), (1, X_COL)):
        over_peers(axis, lambda p: copy(pk.at[p // 2], xr.at[axis, place[axis]], group, p, place[axis], peer(axis, p)).start())
        xr[axis, place[axis]] = pk[place[axis] // 2]

    def steer(which):
        loads[which].wait()
        rate = jnp.where(slots[which] // 4 == 0, RATES[0], RATES[1]).astype(F32)

        def step(q, carry):
            turns = dbuf[which, pl.ds(pl.multiple_of(q * OWN, 8), OWN), :].astype(F32) * rate
            x = turns - jnp.round(turns)
            z = x * x
            pad = jnp.zeros((SLOT - OWN, HALF), F32)
            at = pl.ds(pl.multiple_of(q * SLOT, SLOT), SLOT)
            tab[which, at, :HALF] = jnp.concatenate([horner(COS, z), pad], axis=0).astype(BF16)
            tab[which, at, HALF:] = jnp.concatenate([horner(SIN, z) * x, pad], axis=0).astype(BF16)
            return carry

        lax.fori_loop(0, SIDE, step, 0)

    steer(0)
    over_peers(0, lambda p: copy(pw_send, pw.at[0, p], PW_ROW, p, p, peer(0, p)).wait_recv())
    lv_tile = jnp.sum(pw[0], axis=0)
    lv_send[...] = lv_tile
    over_peers(1, lambda p: copy(lv_send, lv.at[r], LV_COL, p, r, peer(1, p)).start())
    lv[r] = lv_tile
    steer(1)
    over_peers(1, lambda p: copy(pw_send, pw.at[1, p], PW_COL, p, p, peer(1, p)).wait_recv())
    for axis, group in ((0, X_ROW), (1, X_COL)):
        over_peers(axis, lambda p: copy(pk.at[0], xr.at[axis, p], group, p, p, peer(axis, p)).wait_recv())
    over_peers(1, lambda p: copy(lv_send, lv.at[p], LV_COL, p, p, peer(1, p)).wait_recv())
    level = 0.5 * jnp.sum(lv[...], axis=0)

    for which, group in ((0, SUM_U), (1, SUM_V)):
        first = slots[which] // 4 == 0
        power = jnp.where(first, pw[which, :, 0, :], pw[which, :, 1, :])
        lev = jnp.where(first, level[2:3], level[3:4])
        used = lax.broadcasted_iota(jnp.int32, (SIDE, 128), 1) < OWN
        gain = jnp.where(used, lax.rsqrt(power + lev), 0.0)
        gain = jnp.concatenate([gain, jnp.zeros((128 - SIDE, 128), F32)], axis=0).T[:SLOT]
        scaled = jnp.concatenate(
            [(xr[which, q].astype(F32) * gain[:, q : q + 1]).astype(BF16) for q in range(SIDE)], axis=0
        )
        sums_t = lax.dot_general(
            scaled, tab[which], (((0,), (0,)), ((), ())), preferred_element_type=F32
        )
        re = sums_t[:64, :HALF] - sums_t[64:, HALF:]
        im = sums_t[64:, :HALF] + sums_t[:64, HALF:]
        value = jnp.concatenate([re, im], axis=0)
        for h in range(2):
            turned = value[:, 128 * h : 128 * h + 128].T.astype(BF16)
            for j in range(4):
                sums[which, 4 * h + j] = turned[BEAMS * j : BEAMS * j + BEAMS]
        other = 1 - which
        mine = place[other]

        def send_sum(j, carry):
            target = halves[which] * 8 + j

            @pl.when(target != mine)
            def _():
                copy(sums.at[which, j], part.at[which, mine], group, j, mine, peer(other, target)).start()

            return carry

        lax.fori_loop(0, 8, send_sum, 0)

        @pl.when(holder[which])
        def _():
            part[which, mine] = sums[which, lax.rem(mine, 8)]

    for which, group, after in ((0, SUM_U, ALL_U), (1, SUM_V, ALL_V)):
        other = 1 - which

        @pl.when(holder[which])
        def _():
            over_peers(other, lambda p: copy(sums.at[which, 0], part.at[which, p], group, 0, p, peer(other, p)).wait_recv())
            total = jnp.sum(part[which].astype(F32), axis=0).astype(BF16)
            block[which] = total
            over_peers(
                which,
                lambda p: copy(
                    block.at[which], gathered.at[which, slots[which]], after, p, slots[which], peer(which, p)
                ).start(),
            )
            gathered[which, slots[which]] = total

    for which, after in ((0, ALL_U), (1, ALL_V)):
        half_here = rank[which] // 8

        def arrive(s, carry):
            @pl.when(2 * s + half_here != place[which])
            def _():
                copy(block.at[which], gathered.at[which, s], after, 0, s, peer(which, 2 * s + half_here)).wait_recv()

            return carry

        lax.fori_loop(0, 8, arrive, 0)

    low = lax.broadcasted_iota(jnp.int32, (BEAMS, 128), 1) < 64
    for f in range(2):
        acc = jnp.zeros((BEAMS, 2 * BEAMS), F32)
        for k in range(4):
            u = gathered[0, 4 * f + k]
            turned = pltpu.roll(u.astype(F32), 64, 1)
            turned = jnp.where(low, turned, -turned).astype(BF16)
            acc += lax.dot_general(
                gathered[1, 4 * f + k], jnp.concatenate([u, turned], axis=0),
                (((1,), (1,)), ((), ())), preferred_element_type=F32,
            )
        acc = acc * (math.sqrt(WINDOWS) / STATIONS)
        out[f, 0] = acc[:, :BEAMS]
        out[f, 1] = acc[:, BEAMS:]

    for axis, a, b, d in ((0, PW_ROW, X_ROW, None), (1, PW_COL, X_COL, LV_COL)):
        over_peers(axis, lambda p: copy(pw_send, pw.at[axis, p], a, p, p, peer(axis, p)).wait_send())
        over_peers(axis, lambda p: copy(pk.at[0], xr.at[axis, p], b, p, p, peer(axis, p)).wait_send())
        if d is not None:
            over_peers(axis, lambda p: copy(lv_send, lv.at[p], d, p, p, peer(axis, p)).wait_send())
    for which, group, after in ((0, SUM_U, ALL_U), (1, SUM_V, ALL_V)):
        other = 1 - which

        def sent(j, carry):
            target = halves[which] * 8 + j

            @pl.when(target != place[other])
            def _():
                copy(sums.at[which, j], part.at[which, 0], group, j, 0, peer(other, target)).wait_send()

            return carry

        lax.fori_loop(0, 8, sent, 0)

        @pl.when(holder[which])
        def _():
            over_peers(which, lambda p: copy(block.at[which], gathered.at[which, 0], after, p, 0, peer(which, p)).wait_send())


def body(spectra, delays_s, delays_r, wl_index):
    return pl.pallas_call(
        kernel,
        out_shape=jax.ShapeDtypeStruct((2, 2, BEAMS, BEAMS), F32),
        in_specs=[pl.BlockSpec(memory_space=pl.ANY)] * 3 + [pl.BlockSpec(memory_space=pltpu.SMEM)],
        out_specs=pl.BlockSpec(memory_space=pltpu.VMEM),
        scratch_shapes=[
            pltpu.VMEM((2, 2, OWN, WINDOWS), BF16),
            pltpu.VMEM((2, SIDE * OWN, HALF), jnp.int32),
            pltpu.VMEM((2, SIDE * SLOT, 2 * HALF), BF16),
            pltpu.VMEM((8, SLOT, 128), BF16),
            pltpu.VMEM((2, SIDE, SLOT, 128), BF16),
            pltpu.VMEM((8, 128), F32),
            pltpu.VMEM((2, SIDE, 8, 128), F32),
            pltpu.VMEM((8, 128), F32),
            pltpu.VMEM((SIDE, 8, 128), F32),
            pltpu.VMEM((2, 8, BEAMS, 128), BF16),
            pltpu.VMEM((2, SIDE, BEAMS, 128), BF16),
            pltpu.VMEM((2, BEAMS, 128), BF16),
            pltpu.VMEM((2, 8, BEAMS, 128), BF16),
            pltpu.SemaphoreType.DMA((3,)),
            pltpu.SemaphoreType.DMA((9, SIDE)),
            pltpu.SemaphoreType.DMA((9, SIDE)),
        ],
        compiler_params=pltpu.CompilerParams(collective_id=0, has_side_effects=True),
    )(spectra, delays_s, delays_r, wl_index)


def solution(mesh):
    in_specs = (P(None, None, ("row", "col"), None), P("row", None), P("col", None), P())
    out_specs = P(None, None, "col", "row")
    return jax.shard_map(body, mesh=mesh, in_specs=in_specs, out_specs=out_specs, check_vma=False)
```

profile of v0, /device:TPU:1, one launch (start us, length us, event | category | flops | bytes accessed | tf_op | source)
XLA Modules:
  0.0 41.8 jit_solution(12728685290422106564)
XLA Ops:
  0.0 40.3 %shard_map.46 = f32[2,2,32,32]{3,2,1,0:T(8,128)} custom-call(bf16[2,2,40,256]{3,2,1,0:T(8,128)(2,1)} %spec_hbm.1, s32[640,512]{1,0:T(8,128)} %ds_hbm.1, s32[640,512]{1,0:T(8,128)} %dr_hbm.1, s32[2]{0:T(128)} %wl.1), custom_call_target="tpu_custom_call" | custom-call | tf_op jit(solution)/shard_map/pallas_call | solution.py:245
  40.3 1.5 %copy.6 = f32[2,2,32,32]{3,2,1,0:T(8,128)} copy(f32[2,2,32,32]{3,2,1,0:T(8,128)} %shard_map.46) | data formatting | bytes 32768
where the time goes:
time: 41.9 us; the launch traced here: 41.8 us
  Pallas kernels  40.3 us (96%)
  local copies, waits for them, and re-layouts  1.47 us (4%)
    pallas_call x1, Pallas kernels, body(): pl.pallas_call(kernel, out_shape=jax.ShapeDtypeStruct((2, 2, BEAMS, BEAMS...  40.3 us
    unnamed x1, local copies, waits for them, and re-layouts  1.47 us

commit v1 on v0

v1 whole, which is shorter than its diff:
```python
import functools
import math

import jax
import jax.numpy as jnp
from jax import lax
from jax.experimental import pallas as pl
from jax.experimental.pallas import tpu as pltpu
from jax.sharding import PartitionSpec as P

MESH = pl.DeviceIdType.MESH
F32 = jnp.float32
BF16 = jnp.bfloat16

STATIONS = 10240
WINDOWS = 256
SIDE = 16
OWN = 40
SLOT = 48
HALF = 256
BEAMS = 32
RATES = (0.0361, 0.0596)

COS = (0.9999992215668542, -19.7389825153523, 64.92872658489378, -85.27239662504564, 58.79403695210448, -21.076779298561963)
SIN = (6.283182818541802, -41.34142139793358, 81.59618385577838, -76.58010036540968, 41.20539421297601, -12.271261390344423)

PW, X_ROW, X_COL, LV, SUM_U, SUM_V, ALL_U, ALL_V = range(8)
MARK = 16


def horner(coefs, z):
    acc = jnp.full_like(z, coefs[-1])
    for c in coefs[-2::-1]:
        acc = acc * z + c
    return acc


def kernel(
    spec_hbm, ds_hbm, dr_hbm, wl, out,
    xin, dbuf, tab, turned, pk, xr, xf, pw_send, pw, lv_send, lv, sums, part, block, gathered,
    load, send, recv,
):
    r, c = lax.axis_index("row"), lax.axis_index("col")
    slots = (c // 2, r // 2)
    halves = (c % 2, r % 2)
    holder = (r // 8 == halves[0], c // 8 == halves[1])
    place = (c, r)
    rank = (r, c)

    def peer(axis, other):
        return (r, other) if axis == 0 else (other, c)

    def copy(src, dst, group, device):
        return pltpu.make_async_remote_copy(
            src_ref=src, dst_ref=dst, send_sem=send.at[group], recv_sem=recv.at[group],
            device_id=device, device_id_type=MESH,
        )

    def over_peers(axis, action):
        def step(o, carry):
            action(lax.rem(place[axis] + o, SIDE))
            return carry

        lax.fori_loop(1, SIDE, step, 0)

    def arrived(ref, n, group):
        copy(ref.at[pl.ds(0, n)], ref.at[pl.ds(0, n)], group, (r, c)).wait_recv()

    def left(ref, n, group):
        copy(ref.at[pl.ds(0, n)], ref.at[pl.ds(0, n)], group, (r, c)).wait_send()

    def load_delays(hbm, which):
        start = pl.multiple_of(halves[which] * HALF, HALF)
        return pltpu.make_async_copy(hbm.at[:, pl.ds(start, HALF)], dbuf.at[which], load.at[which])

    loads = [load_delays(ds_hbm, 0), load_delays(dr_hbm, 1)]
    load_x = pltpu.make_async_copy(spec_hbm, xin, load.at[2])
    load_x.start()
    for item in loads:
        item.start()
    barrier = pltpu.get_barrier_semaphore()
    for axis in (0, 1):
        over_peers(axis, lambda p: pl.semaphore_signal(barrier, inc=1, device_id=peer(axis, p), device_id_type=MESH))

    load_x.wait()
    tiles = [[[xin[f, p, :, 128 * t : 128 * t + 128].astype(F32) for t in range(2)] for p in range(2)] for f in range(2)]
    lane = lax.broadcasted_iota(jnp.int32, (8, 128), 1)
    station = (r * SIDE + c) * OWN + lax.broadcasted_iota(jnp.int32, (8, 128), 0)
    power, marked = [], jnp.zeros((8, 128), F32)
    for f in range(2):
        total = sum(tiles[f][p][t] * tiles[f][p][t] for p in range(2) for t in range(2))
        column = jnp.sum(total, axis=1, keepdims=True)
        tile = jnp.zeros((8, 128), F32)
        for j in range(5):
            own = column[8 * j : 8 * j + 8]
            tile = jnp.where(lane == j, own, tile)
            marked = jnp.where((lane == MARK + 5 * f + j) & (station + 8 * j == wl[f]), own, marked)
        power.append(tile)
    for f in range(2):
        pw_send[f] = power[f] + marked

    pl.semaphore_wait(barrier, 2 * (SIDE - 1))

    over_peers(0, lambda p: copy(pw_send.at[p // 8], pw.at[c], PW, peer(0, p)).start())
    pw[c] = pw_send[c // 8]

    low = lax.broadcasted_iota(jnp.int32, (OWN, 128), 1) < 64
    for f in range(2):
        for t in range(2):
            re, im = tiles[f][0][t], tiles[f][1][t]
            first = jnp.where(low, re, pltpu.roll(im, 64, 1))
            second = jnp.where(low, pltpu.roll(re, 64, 1), im)
            for k, value in ((2 * t, first), (2 * t + 1, second)):
                pk[4 * f + k] = jnp.concatenate([value, jnp.zeros((SLOT - OWN, 128), F32)], axis=0).astype(BF16)
    for axis, group in ((1, X_COL), (0, X_ROW)):
        over_peers(axis, lambda p: copy(pk.at[p // 2], xr.at[axis, place[axis]], group, peer(axis, p)).start())
        xr[axis, place[axis]] = pk[place[axis] // 2]

    def steer(which):
        loads[which].wait()
        rate = jnp.where(slots[which] // 4 == 0, RATES[0], RATES[1]).astype(F32)

        def step(q, carry):
            turns = dbuf[which, pl.ds(pl.multiple_of(q * OWN, 8), OWN), :].astype(F32) * rate
            x = turns - jnp.round(turns)
            z = x * x
            pad = jnp.zeros((SLOT - OWN, HALF), F32)
            at = pl.ds(pl.multiple_of(q * SLOT, SLOT), SLOT)
            tab[at, :HALF] = jnp.concatenate([horner(COS, z), pad], axis=0).astype(BF16)
            tab[at, HALF:] = jnp.concatenate([horner(SIN, z) * x, pad], axis=0).astype(BF16)
            return carry

        lax.fori_loop(0, SIDE, step, 0)
        for h in range(2):
            for b in range(SIDE * SLOT // 128):
                turned[which, :, SIDE * SLOT * h + 128 * b : SIDE * SLOT * h + 128 * b + 128] = tab[
                    128 * b : 128 * b + 128, HALF * h : HALF * h + HALF
                ].T

    steer(0)
    arrived(pw, SIDE - 1, PW)
    mark = jnp.where(lane >= MARK, jnp.sum(pw[...], axis=0), 0.0)
    for f in range(2):
        lv_send[f] = jnp.where(lane < MARK, power[f], mark)
    over_peers(1, lambda p: copy(lv_send.at[p // 8], lv.at[r], LV, peer(1, p)).start())
    lv[r] = lv_send[r // 8]
    steer(1)

    low = lax.broadcasted_iota(jnp.int32, (SLOT, 128), 1) < 64
    for axis, group in ((0, X_ROW), (1, X_COL)):
        arrived(xr.at[axis], SIDE - 1, group)

        def unpack(q, carry):
            x = xr[axis, q].astype(F32)
            at = pl.ds(pl.multiple_of(q * SLOT, SLOT), SLOT)
            xf[axis, 0, at] = x
            x = pltpu.roll(x, 64, 1)
            xf[axis, 1, at] = jnp.where(low, -x, x)
            return carry

        lax.fori_loop(0, SIDE, unpack, 0)
    arrived(lv, SIDE - 1, LV)
    mark = jnp.sum(lv[...], axis=0)

    for which, group, source in ((0, SUM_U, pw), (1, SUM_V, lv)):
        start = MARK + 5 * (slots[which] // 4)
        level = 0.5 * jnp.sum(jnp.where((lane >= start) & (lane < start + 5), mark, 0.0), keepdims=True)
        scaled = [[], []]
        for q in range(SIDE):
            gain = lax.rsqrt(source[q] + level)
            gain = jnp.concatenate([gain[:, j : j + 1] for j in range(5)] + [jnp.zeros((8, 1), F32)], axis=0)
            for side in range(2):
                scaled[side].append((xf[which, side, SLOT * q : SLOT * q + SLOT] * gain).astype(BF16))
        value = jnp.dot(
            turned[which], jnp.concatenate(scaled[0] + scaled[1], axis=0), preferred_element_type=F32
        ).astype(BF16)
        for j in range(8):
            sums[which, j] = value[BEAMS * j : BEAMS * j + BEAMS]
        other = 1 - which
        mine = place[other]

        def send_sum(j, carry):
            target = halves[which] * 8 + j

            @pl.when(target != mine)
            def _():
                copy(sums.at[which, j], part.at[which, mine], group, peer(other, target)).start()

            return carry

        lax.fori_loop(0, 8, send_sum, 0)

        @pl.when(holder[which])
        def _():
            part[which, mine] = sums[which, lax.rem(mine, 8)]

    for which, group, after in ((1, SUM_V, ALL_V), (0, SUM_U, ALL_U)):

        @pl.when(holder[which])
        def _():
            arrived(part.at[which], SIDE - 1, group)
            total = jnp.sum(part[which].astype(F32), axis=0).astype(BF16)
            block[which] = total
            over_peers(
                which,
                lambda p: copy(block.at[which], gathered.at[which, slots[which]], after, peer(which, p)).start(),
            )
            gathered[which, slots[which]] = total

    for which, after in ((0, ALL_U), (1, ALL_V)):

        @pl.when(holder[which])
        def _():
            arrived(gathered.at[which], 7, after)

        @pl.when(jnp.logical_not(holder[which]))
        def _():
            arrived(gathered.at[which], 8, after)

    low = lax.broadcasted_iota(jnp.int32, (BEAMS, 128), 1) < 64
    for f in range(2):
        acc = jnp.zeros((BEAMS, 2 * BEAMS), F32)
        for k in range(4):
            u = gathered[0, 4 * f + k]
            swapped = pltpu.roll(u.astype(F32), 64, 1)
            swapped = jnp.where(low, swapped, -swapped).astype(BF16)
            acc += lax.dot_general(
                gathered[1, 4 * f + k], jnp.concatenate([u, swapped], axis=0),
                (((1,), (1,)), ((), ())), preferred_element_type=F32,
            )
        acc = acc * (math.sqrt(WINDOWS) / STATIONS)
        out[f, 0] = acc[:, :BEAMS]
        out[f, 1] = acc[:, BEAMS:]

    left(pw, SIDE - 1, PW)
    left(xr.at[0], SIDE - 1, X_ROW)
    left(xr.at[1], SIDE - 1, X_COL)
    left(lv, SIDE - 1, LV)
    for which, group, after in ((0, SUM_U, ALL_U), (1, SUM_V, ALL_V)):

        @pl.when(holder[which])
        def _():
            left(part.at[which], 7, group)
            left(part.at[which], SIDE - 1, after)

        @pl.when(jnp.logical_not(holder[which]))
        def _():
            left(part.at[which], 8, group)


def body(spectra, delays_s, delays_r, wl_index):
    return pl.pallas_call(
        kernel,
        out_shape=pltpu.VMEM((2, 2, BEAMS, BEAMS), F32),
        in_specs=[pl.BlockSpec(memory_space=pl.ANY)] * 3 + [pl.BlockSpec(memory_space=pltpu.SMEM)],
        out_specs=pl.BlockSpec(memory_space=pltpu.VMEM),
        scratch_shapes=[
            pltpu.VMEM((2, 2, OWN, WINDOWS), BF16),
            pltpu.VMEM((2, SIDE * OWN, HALF), jnp.int32),
            pltpu.VMEM((SIDE * SLOT, 2 * HALF), BF16),
            pltpu.VMEM((2, HALF, 2 * SIDE * SLOT), BF16),
            pltpu.VMEM((8, SLOT, 128), BF16),
            pltpu.VMEM((2, SIDE, SLOT, 128), BF16),
            pltpu.VMEM((2, 2, SIDE * SLOT, 128), F32),
            pltpu.VMEM((2, 8, 128), F32),
            pltpu.VMEM((SIDE, 8, 128), F32),
            pltpu.VMEM((2, 8, 128), F32),
            pltpu.VMEM((SIDE, 8, 128), F32),
            pltpu.VMEM((2, 8, BEAMS, 128), BF16),
            pltpu.VMEM((2, SIDE, BEAMS, 128), BF16),
            pltpu.VMEM((2, BEAMS, 128), BF16),
            pltpu.VMEM((2, 8, BEAMS, 128), BF16),
            pltpu.SemaphoreType.DMA((3,)),
            pltpu.SemaphoreType.DMA((8,)),
            pltpu.SemaphoreType.DMA((8,)),
        ],
        compiler_params=pltpu.CompilerParams(collective_id=0, has_side_effects=True),
    )(spectra, delays_s, delays_r, wl_index)


def solution(mesh):
    in_specs = (P(None, None, ("row", "col"), None), P("row", None), P("col", None), P())
    out_specs = P(None, None, "col", "row")
    return jax.shard_map(body, mesh=mesh, in_specs=in_specs, out_specs=out_specs, check_vma=False)
```

time: 41.9 us -> 36.3 us (0.87)
  Pallas kernels: 40.3 us -> 35.6 us
  local copies, waits for them, and re-layouts: 1.47 us -> 0.63 us
    pallas_call x1, Pallas kernels: 40.3 us -> 35.6 us  [body(): pl.pallas_call(kernel, out_shape=pltpu.VMEM((2, 2, BEAMS, BEAMS), F32), i...]
    unnamed x1, local copies, waits for them, and re-layouts: 1.47 us -> 0.63 us
where the time goes in v1:
time: 36.3 us; the launch traced here: 36.2 us
  Pallas kernels  35.6 us (98%)
  local copies, waits for them, and re-layouts  0.63 us (2%)
    pallas_call x1, Pallas kernels, body(): pl.pallas_call(kernel, out_shape=pltpu.VMEM((2, 2, BEAMS, BEAMS), F32), i...  35.6 us

profile of v1, /device:TPU:1, one launch (start us, length us, event | category | flops | bytes accessed | tf_op | source)
XLA Modules:
  0.0 36.2 jit_solution(3863223312721650513)
XLA Ops:
  0.0 35.6 %shard_map.46 = f32[2,2,32,32]{3,2,1,0:T(8,128)S(1)} custom-call(bf16[2,2,40,256]{3,2,1,0:T(8,128)(2,1)} %spec_hbm.1, s32[640,512]{1,0:T(8,128)} %ds_hbm.1, s32[640,512]{1,0:T(8,128)} %dr_hbm.1, s32[2]{0:T(128)} %wl.1), custom_call_target="tpu_custom_call" | custom-call | tf_op jit(solution)/shard_map/pallas_call | solution.py:252
  35.6 0.6 %copy.6 = f32[2,2,32,32]{3,2,1,0:T(8,128)} copy(f32[2,2,32,32]{3,2,1,0:T(8,128)S(1)} %shard_map.46) | data formatting | bytes 32768

commit v2 on v1

v2 whole, which is shorter than its diff:
```python
import functools
import math

import jax
import jax.numpy as jnp
from jax import lax
from jax.experimental import pallas as pl
from jax.experimental.pallas import tpu as pltpu
from jax.sharding import PartitionSpec as P

MESH = pl.DeviceIdType.MESH
F32 = jnp.float32
BF16 = jnp.bfloat16

STATIONS = 10240
WINDOWS = 256
SIDE = 16
OWN = 40
SLOT = 48
HALF = 256
BEAMS = 32
RATES = (0.0361, 0.0596)

COS = (0.9999992215668542, -19.7389825153523, 64.92872658489378, -85.27239662504564, 58.79403695210448, -21.076779298561963)
SIN = (6.283182818541802, -41.34142139793358, 81.59618385577838, -76.58010036540968, 41.20539421297601, -12.271261390344423)

PW, X_ROW, X_CORE, X_COL, LV, SUM_U, SUM_V, ALL_U, ALL_V = range(9)
RINGS = ((4, 3, 5, 2, 6, 1, 7, 0), (2, 1, 3, 0))
MARK = OWN


def horner(coefs, z):
    acc = jnp.full_like(z, coefs[-1])
    for c in coefs[-2::-1]:
        acc = acc * z + c
    return acc


def kernel(
    spec_hbm, ds_hbm, dr_hbm, wl, out,
    xin, dbuf, tab, turned, pk, xr, xf, pw_send, pw, powers, lv_send, lv, sums, part, block, gathered, right,
    load, send, recv,
):
    r, c = lax.axis_index("row"), lax.axis_index("col")
    slots = (c // 2, r // 2)
    halves = (c % 2, r % 2)
    holder = (r // 8 == halves[0], c // 8 == halves[1])
    place = (c, r)
    rank = (r, c)

    def peer(axis, other):
        return (r, other) if axis == 0 else (other, c)

    (y_lo, z), (y_hi, x, core) = (r // 8, r % 8), (c // 8, c // 2 % 4, c % 2)
    zs = {d: lax.rem(z + d, 8) for d in RINGS[0]}
    xs = {d: lax.rem(x + d, 4) * 2 for d in RINGS[1]}
    flip = lambda bit, d: 1 - bit if d else bit
    hops = lambda d, n: min(d, n - d)
    others = ([], [])
    for dx, dy, dc in sorted(
        ((dx, dy, dc) for dx in RINGS[1] for dy in (1, 0) for dc in (1, 0)), key=lambda d: -hops(d[0], 4) - 2 * d[1]
    ):
        if dx or dy or dc:
            f = flip(y_hi, dy)
            others[0].append((hops(dx, 4) + 2 * dy, f * 8 + xs[dx] + flip(core, dc), f, f * 4 + lax.div(xs[dx], 2), dc))
    for dz, dy in sorted(((dz, dy) for dz in RINGS[0] for dy in (1, 0)), key=lambda d: -hops(d[0], 8) - d[1]):
        if dz or dy:
            f = flip(y_lo, dy)
            others[1].append((hops(dz, 8) + dy, f * 8 + zs[dz], f, f * 4 + lax.div(zs[dz], 2), 0))

    def copy(src, dst, group, device):
        return pltpu.make_async_remote_copy(
            src_ref=src, dst_ref=dst, send_sem=send.at[group], recv_sem=recv.at[group],
            device_id=device, device_id_type=MESH,
        )

    def arrived(ref, n, group):
        copy(ref.at[pl.ds(0, n)], ref.at[pl.ds(0, n)], group, (r, c)).wait_recv()

    def left(ref, n, group):
        copy(ref.at[pl.ds(0, n)], ref.at[pl.ds(0, n)], group, (r, c)).wait_send()

    def load_delays(hbm, which):
        start = pl.multiple_of(halves[which] * HALF, HALF)
        return pltpu.make_async_copy(hbm.at[:, pl.ds(start, HALF)], dbuf.at[which], load.at[which])

    loads = [load_delays(ds_hbm, 0), load_delays(dr_hbm, 1)]
    load_x = pltpu.make_async_copy(spec_hbm, xin, load.at[2])
    load_x.start()
    for item in loads:
        item.start()
    barrier = pltpu.get_barrier_semaphore()
    for _, axis, p in sorted(((-item[0], axis, k) for axis in (1, 0) for k, item in enumerate(others[axis]))):
        pl.semaphore_signal(barrier, inc=1, device_id=peer(axis, others[axis][p][1]), device_id_type=MESH)

    load_x.wait()
    tiles = [[[xin[f, p, :, 128 * t : 128 * t + 128].astype(F32) for t in range(2)] for p in range(2)] for f in range(2)]
    lane = lax.broadcasted_iota(jnp.int32, (1, 128), 1)
    column = jnp.zeros((OWN, 128), F32)
    for f in range(2):
        total = sum(tiles[f][p][t] * tiles[f][p][t] for p in range(2) for t in range(2))
        at = lax.broadcasted_iota(jnp.int32, (OWN, 128), 1)
        column = jnp.where(at == f, jnp.sum(total, axis=1, keepdims=True), column)
    rows = jnp.concatenate([column, jnp.zeros((128 - OWN, 128), F32)], axis=0).T
    power = [rows[f : f + 1] for f in range(2)]
    station = (r * SIDE + c) * OWN + lane
    marked = jnp.zeros((1, 128), F32)
    for f in range(2):
        mine = (station == wl[f]) & (lane < OWN)
        marked = jnp.where(lane == MARK + f, jnp.sum(jnp.where(mine, power[f], 0.0), axis=1, keepdims=True), marked)
    for f in range(2):
        pw_send[f, :1] = jnp.where(lane < OWN, power[f], marked)

    pl.semaphore_wait(barrier, 2 * (SIDE - 1))

    for _, p, f, _, _ in others[0]:
        copy(pw_send.at[f, pl.ds(0, 1)], pw.at[c, pl.ds(0, 1)], PW, peer(0, p)).start()
    pw[c, :1] = pw_send[c // 8, :1]

    low = lax.broadcasted_iota(jnp.int32, (OWN, 128), 1) < 64
    for f in range(2):
        for t in range(2):
            re, im = tiles[f][0][t], tiles[f][1][t]
            first = jnp.where(low, re, pltpu.roll(im, 64, 1))
            second = jnp.where(low, pltpu.roll(re, 64, 1), im)
            for k, value in ((2 * t, first), (2 * t + 1, second)):
                pk[4 * f + k] = jnp.concatenate([value, jnp.zeros((SLOT - OWN, 128), F32)], axis=0).astype(BF16)
    used = pl.ds(0, OWN)
    at = (core * 8 + c // 2, r)
    for axis, group in ((1, X_COL), (0, X_ROW)):
        for _, p, _, slot, cross in others[axis]:
            if not cross:
                copy(pk.at[slot, used], xr.at[axis, at[axis], used], group, peer(axis, p)).start()
        xr[axis, at[axis]] = pk[place[axis] // 2]

    def steer(which):
        loads[which].wait()
        rate = jnp.where(slots[which] // 4 == 0, RATES[0], RATES[1]).astype(F32)

        def step(q, carry):
            turns = dbuf[which, pl.ds(pl.multiple_of(q * OWN, 8), OWN), :].astype(F32) * rate
            x = turns - jnp.round(turns)
            z = x * x
            pad = jnp.zeros((SLOT - OWN, HALF), F32)
            n = q % 2 * 8 + q // 2 if which == 0 else q
            at = pl.ds(pl.multiple_of(n * SLOT, SLOT), SLOT)
            tab[at, :HALF] = jnp.concatenate([horner(COS, z), pad], axis=0).astype(BF16)
            tab[at, HALF:] = jnp.concatenate([horner(SIN, z) * x, pad], axis=0).astype(BF16)
            return carry

        lax.fori_loop(0, SIDE, step, 0)
        for h in range(2):
            for b in range(SIDE * SLOT // 128):
                turned[which, HALF * h : HALF * h + HALF, 128 * b : 128 * b + 128] = tab[
                    128 * b : 128 * b + 128, HALF * h : HALF * h + HALF
                ].T

    def columns(ref):
        return jnp.concatenate([ref[:, 0, :], jnp.zeros((128 - SIDE, 128), F32)], axis=0).T[:SLOT]

    steer(0)
    arrived(pw.at[:, pl.ds(0, 1)], SIDE - 1, PW)
    mark = jnp.sum(pw[:, 0, :], axis=0, keepdims=True)
    for f in range(2):
        lv_send[f, :1] = jnp.where(lane < OWN, power[f], mark)
    for _, p, f, _, _ in others[1]:
        copy(lv_send.at[f, pl.ds(0, 1)], lv.at[r, pl.ds(0, 1)], LV, peer(1, p)).start()
    lv[r, :1] = lv_send[r // 8, :1]

    arrived(xr.at[0, :, used], 7, X_ROW)
    half = xr.at[0, pl.ds(core * 8, 8), used]
    copy(half, half, X_CORE, peer(0, c + 1 - 2 * core)).start()
    powers[...] = columns(pw)
    steer(1)

    def unpack(axis):
        def step(n, carry):
            at = pl.ds(pl.multiple_of(n * SLOT, SLOT), SLOT)
            xf[axis, at] = jnp.concatenate(
                [xr[axis, n, :OWN].astype(F32), jnp.zeros((SLOT - OWN, 128), F32)], axis=0
            )
            return carry

        lax.fori_loop(0, SIDE, step, 0)

    arrived(xr.at[1, :, used], SIDE - 1, X_COL)
    unpack(1)
    arrived(xr.at[0, :, used], 8, X_CORE)
    unpack(0)
    arrived(lv.at[:, pl.ds(0, 1)], SIDE - 1, LV)
    mark = jnp.sum(lv[:, 0, :], axis=0, keepdims=True)
    station = lax.broadcasted_iota(jnp.int32, (SLOT, 128), 0)
    low = lax.broadcasted_iota(jnp.int32, (HALF, 128), 1) < 64
    for which in range(2):
        level = 0.5 * jnp.sum(jnp.where(lane == MARK + slots[which] // 4, mark, 0.0), axis=1, keepdims=True)
        gain = jnp.where(station < OWN, lax.rsqrt((powers[...] if which == 0 else columns(lv)) + level), 0.0)
        scaled = []
        for n in range(SIDE):
            q = n % 8 * 2 + n // 8 if which == 0 else n
            scaled.append((xf[which, SLOT * n : SLOT * n + SLOT] * gain[:, q : q + 1]).astype(BF16))
        both = jnp.dot(turned[which], jnp.concatenate(scaled, axis=0), preferred_element_type=F32)
        swapped = pltpu.roll(both[HALF:], 64, 1)
        value = (both[:HALF] + jnp.where(low, -swapped, swapped)).astype(BF16)
        for j in range(8):
            sums[which, j] = value[BEAMS * j : BEAMS * j + BEAMS]

    nears = (
        [zs[d] for d in RINGS[0]],
        [xs[d] + flip(core, dc) for d in RINGS[1] for dc in (1, 0)],
    )
    for which, group in ((0, SUM_U), (1, SUM_V)):
        other = 1 - which

        def send_sum(j):
            copy(sums.at[which, j], part.at[which, place[other]], group, peer(other, halves[which] * 8 + j)).start()

        for j in nears[which][:-1]:
            send_sum(j)
        j = nears[which][-1]

        @pl.when(jnp.logical_not(holder[which]))
        def _():
            send_sum(j)

        @pl.when(holder[which])
        def _():
            part[which, place[other]] = sums[which, j]

    for which, group, after in ((1, SUM_V, ALL_V), (0, SUM_U, ALL_U)):

        @pl.when(holder[which])
        def _():
            arrived(part.at[which], SIDE - 1, group)
            total = jnp.sum(part[which].astype(F32), axis=0).astype(BF16)
            block[which] = total
            for _, p, _, _, _ in others[which]:
                copy(block.at[which], gathered.at[which, slots[which]], after, peer(which, p)).start()
            gathered[which, slots[which]] = total

    def all_arrived(which, group):
        @pl.when(holder[which])
        def _():
            arrived(gathered.at[which], 7, group)

        @pl.when(jnp.logical_not(holder[which]))
        def _():
            arrived(gathered.at[which], 8, group)

    all_arrived(0, ALL_U)
    low = lax.broadcasted_iota(jnp.int32, (BEAMS, 128), 1) < 64
    for k in range(8):
        u = gathered[0, k].astype(F32)
        swapped = pltpu.roll(u, 64, 1)
        swapped = jnp.where(low, swapped, -swapped)
        right[k] = jnp.concatenate([u, swapped, jnp.zeros((64, 128), F32)], axis=0).T.astype(BF16)
    all_arrived(1, ALL_V)
    for f in range(2):
        acc = sum(
            jnp.dot(gathered[1, 4 * f + k], right[4 * f + k], preferred_element_type=F32) for k in range(4)
        ) * (math.sqrt(WINDOWS) / STATIONS)
        out[f, 0] = acc[:, :BEAMS]
        out[f, 1] = acc[:, BEAMS : 2 * BEAMS]

    left(pw.at[:, pl.ds(0, 1)], SIDE - 1, PW)
    left(xr.at[0, :, used], 7, X_ROW)
    left(xr.at[0, :, used], 8, X_CORE)
    left(xr.at[1, :, used], SIDE - 1, X_COL)
    left(lv.at[:, pl.ds(0, 1)], SIDE - 1, LV)
    for which, group, after in ((0, SUM_U, ALL_U), (1, SUM_V, ALL_V)):

        @pl.when(holder[which])
        def _():
            left(part.at[which], 7, group)
            left(part.at[which], SIDE - 1, after)

        @pl.when(jnp.logical_not(holder[which]))
        def _():
            left(part.at[which], 8, group)


def body(spectra, delays_s, delays_r, wl_index):
    return pl.pallas_call(
        kernel,
        out_shape=pltpu.VMEM((2, 2, BEAMS, BEAMS), F32),
        in_specs=[pl.BlockSpec(memory_space=pl.ANY)] * 3 + [pl.BlockSpec(memory_space=pltpu.SMEM)],
        out_specs=pl.BlockSpec(memory_space=pltpu.VMEM),
        scratch_shapes=[
            pltpu.VMEM((2, 2, OWN, WINDOWS), BF16),
            pltpu.VMEM((2, SIDE * OWN, HALF), jnp.int32),
            pltpu.VMEM((SIDE * SLOT, 2 * HALF), BF16),
            pltpu.VMEM((2, 2 * HALF, SIDE * SLOT), BF16),
            pltpu.VMEM((8, SLOT, 128), BF16),
            pltpu.VMEM((2, SIDE, SLOT, 128), BF16),
            pltpu.VMEM((2, SIDE * SLOT, 128), F32),
            pltpu.VMEM((2, 8, 128), F32),
            pltpu.VMEM((SIDE, 8, 128), F32),
            pltpu.VMEM((SLOT, 128), F32),
            pltpu.VMEM((2, 8, 128), F32),
            pltpu.VMEM((SIDE, 8, 128), F32),
            pltpu.VMEM((2, 8, BEAMS, 128), BF16),
            pltpu.VMEM((2, SIDE, BEAMS, 128), BF16),
            pltpu.VMEM((2, BEAMS, 128), BF16),
            pltpu.VMEM((2, 8, BEAMS, 128), BF16),
            pltpu.VMEM((8, 128, 128), BF16),
            pltpu.SemaphoreType.DMA((3,)),
            pltpu.SemaphoreType.DMA((9,)),
            pltpu.SemaphoreType.DMA((9,)),
        ],
        compiler_params=pltpu.CompilerParams(collective_id=0, has_side_effects=True),
    )(spectra, delays_s, delays_r, wl_index)


def solution(mesh):
    in_specs = (P(None, None, ("row", "col"), None), P("row", None), P("col", None), P())
    out_specs = P(None, None, "col", "row")
    return jax.shard_map(body, mesh=mesh, in_specs=in_specs, out_specs=out_specs, check_vma=False)
```

time: 36.3 us -> 32.7 us (0.901)
  Pallas kernels: 35.6 us -> 32 us
    pallas_call x1, Pallas kernels: 35.6 us -> 32 us  [body(): pl.pallas_call(kernel, out_shape=pltpu.VMEM((2, 2, BEAMS, BEAMS), F32), i...]
where the time goes in v2:
time: 32.7 us; the launch traced here: 32.6 us
  Pallas kernels  32 us (98%)
  local copies, waits for them, and re-layouts  0.63 us (2%)
    pallas_call x1, Pallas kernels, body(): pl.pallas_call(kernel, out_shape=pltpu.VMEM((2, 2, BEAMS, BEAMS), F32), i...  32 us

profile of v2, /device:TPU:1, one launch (start us, length us, event | category | flops | bytes accessed | tf_op | source)
XLA Modules:
  0.0 32.6 jit_solution(12483788396375304759)
XLA Ops:
  0.0 32.0 %shard_map.46 = f32[2,2,32,32]{3,2,1,0:T(8,128)S(1)} custom-call(bf16[2,2,40,256]{3,2,1,0:T(8,128)(2,1)} %spec_hbm.1, s32[640,512]{1,0:T(8,128)} %ds_hbm.1, s32[640,512]{1,0:T(8,128)} %dr_hbm.1, s32[2]{0:T(128)} %wl.1), custom_call_target="tpu_custom_call" | custom-call | tf_op jit(solution)/shard_map/pallas_call | solution.py:282
  32.0 0.6 %copy.6 = f32[2,2,32,32]{3,2,1,0:T(8,128)} copy(f32[2,2,32,32]{3,2,1,0:T(8,128)S(1)} %shard_map.46) | data formatting | bytes 32768

commit v3 on v2

v3 whole, which is shorter than its diff:
```python
import functools
import math

import jax
import jax.numpy as jnp
from jax import lax
from jax.experimental import pallas as pl
from jax.experimental.pallas import tpu as pltpu
from jax.sharding import PartitionSpec as P

MESH = pl.DeviceIdType.MESH
F32 = jnp.float32
BF16 = jnp.bfloat16

STATIONS = 10240
WINDOWS = 256
SIDE = 16
OWN = 40
SLOT = 48
HALF = 256
BEAMS = 32
RATES = (0.0361, 0.0596)

COS = (0.9999992215668542, -19.7389825153523, 64.92872658489378, -85.27239662504564, 58.79403695210448, -21.076779298561963)
SIN = (6.283182818541802, -41.34142139793358, 81.59618385577838, -76.58010036540968, 41.20539421297601, -12.271261390344423)

PW, X_ROW, X_CORE, X_COL, X_FAR, X_HAND, LV, SUM_U, SUM_V, ALL_U, ALL_V = range(11)
RINGS = ((4, 3, 5, 2, 6, 1, 7, 0), (2, 1, 3, 0))
MESSAGE = 3


def horner(coefs, z):
    acc = jnp.full_like(z, coefs[-1])
    for c in coefs[-2::-1]:
        acc = acc * z + c
    return acc


def kernel(
    spec_hbm, ds_hbm, dr_hbm, wl, out,
    xin, dbuf_s, dbuf_r, tab, turned_s, turned_r, pk, xr, xf, pw_send, pw, powers, lv_send, lv, sums_s, sums_r, part, block, gathered, right,
    load, send, recv,
):
    r, c = lax.axis_index("row"), lax.axis_index("col")
    (y_lo, z), (y_hi, x, core) = (r // 8, r % 8), (c // 8, c // 2 % 4, c % 2)
    slots = (c // 2, z)
    halves = (core, 1 - y_lo)
    holder = (core != y_lo, core == y_lo)
    across = (1 - y_lo) * 8 + z

    def peer(axis, other):
        return (r, other) if axis == 0 else (other, c)

    zs = {d: lax.rem(z + d, 8) for d in RINGS[0]}
    xs = {d: lax.rem(x + d, 4) * 2 for d in RINGS[1]}
    flip = lambda bit, d: 1 - bit if d else bit
    hops = lambda d, n: min(d, n - d)
    others, facing = ([], []), []
    for dx, dy, dc in sorted(
        ((dx, dy, dc) for dx in RINGS[1] for dy in (1, 0) for dc in (1, 0)), key=lambda d: -hops(d[0], 4) - 2 * d[1]
    ):
        y = flip(y_hi, dy)
        p = y * 8 + xs[dx] + flip(core, dc)
        if dx or dy or dc:
            others[0].append((hops(dx, 4) + 2 * dy, p, y * 4 + lax.div(xs[dx], 2), dc, False))
        facing.append((hops(dx, 4) + 1, p))
    facing.sort(key=lambda item: -item[0])
    for dz, dy in sorted(((dz, dy) for dz in RINGS[0] for dy in (1, 0)), key=lambda d: -hops(d[0], 8) - d[1]):
        if dz or dy:
            others[1].append((hops(dz, 8) + dy, flip(y_lo, dy) * 8 + zs[dz], zs[dz], dy, hops(dz, 8) > 2))

    def copy(src, dst, group, device):
        return pltpu.make_async_remote_copy(
            src_ref=src, dst_ref=dst, send_sem=send.at[group], recv_sem=recv.at[group],
            device_id=device, device_id_type=MESH,
        )

    def arrived(ref, n, group):
        copy(ref.at[pl.ds(0, n)], ref.at[pl.ds(0, n)], group, (r, c)).wait_recv()

    def left(ref, n, group):
        copy(ref.at[pl.ds(0, n)], ref.at[pl.ds(0, n)], group, (r, c)).wait_send()

    start = pl.multiple_of(halves[0] * HALF, HALF)
    loads = [
        pltpu.make_async_copy(ds_hbm.at[:, pl.ds(start, HALF)], dbuf_s, load.at[0]),
        pltpu.make_async_copy(dr_hbm, dbuf_r, load.at[1]),
    ]
    load_x = pltpu.make_async_copy(spec_hbm, xin, load.at[2])
    load_x.start()
    for item in loads:
        item.start()
    row = pl.ds(0, MESSAGE)
    barrier = pltpu.get_barrier_semaphore()
    plane = [(hop, (r, p)) for hop, p, *_ in others[0]] + [(hop, (across, p)) for hop, p in facing]
    column = [(hop, (p, c)) for hop, p, slot, dy, far in others[1] if not (dy and (far or hop == 1))]
    farthest = lambda devices: [device for _, device in sorted(devices, key=lambda item: -item[0])]
    greeted = farthest(plane + column)
    for device in greeted:
        pl.semaphore_signal(barrier, inc=1, device_id=device, device_id_type=MESH)

    pw_send[...] = jnp.zeros((8, 128), F32)
    load_x.wait()
    tiles = [[[xin[f, p, :, 128 * t : 128 * t + 128].astype(F32) for t in range(2)] for p in range(2)] for f in range(2)]
    lane = lax.broadcasted_iota(jnp.int32, (1, 128), 1)
    column = jnp.zeros((OWN, 128), F32)
    for f in range(2):
        total = sum(tiles[f][p][t] * tiles[f][p][t] for p in range(2) for t in range(2))
        at = lax.broadcasted_iota(jnp.int32, (OWN, 128), 1)
        column = jnp.where(at == f, jnp.sum(total, axis=1, keepdims=True), column)
    rows = jnp.concatenate([column, jnp.zeros((128 - OWN, 128), F32)], axis=0).T
    power = [rows[f : f + 1] for f in range(2)]
    station = (r * SIDE + c) * OWN + lane
    pw_send[:1] = power[0] + pltpu.roll(power[1], OWN, 1)
    for f in range(2):
        mine = (station == wl[f]) & (lane < OWN)
        found = jnp.sum(jnp.where(mine, power[f], 0.0), axis=1, keepdims=True)
        pw_send[1 + f : 2 + f] = jnp.broadcast_to(found, (1, 128))

    pl.semaphore_wait(barrier, len(greeted))

    for device in farthest(plane):
        copy(pw_send.at[row], pw.at[y_lo * SIDE + c, row], PW, device).start()
    pw[y_lo * SIDE + c] = pw_send[...]

    low = lax.broadcasted_iota(jnp.int32, (OWN, 128), 1) < 64
    for f in range(2):
        for t in range(2):
            re, im = tiles[f][0][t], tiles[f][1][t]
            first = jnp.where(low, re, pltpu.roll(im, 64, 1))
            second = jnp.where(low, pltpu.roll(re, 64, 1), im)
            for k, value in ((2 * t, first), (2 * t + 1, second)):
                pk[4 * f + k] = jnp.concatenate([value, jnp.zeros((SLOT - OWN, 128), F32)], axis=0).astype(BF16)
    used = pl.ds(0, OWN)
    for _, p, slot, dy, far in others[1]:
        if not (far and dy):
            copy(pk.at[slot, used], xr.at[1, 8 * dy + z, used], X_FAR if far else X_COL, peer(1, p)).start()
    xr[1, z] = pk[slots[1]]
    for _, p, slot, cross, _ in others[0]:
        if not cross:
            copy(pk.at[slot, used], xr.at[0, core * 8 + c // 2, used], X_ROW, peer(0, p)).start()
    xr[0, core * 8 + c // 2] = pk[slots[0]]

    def steer(which):
        loads[which].wait()
        rate = jnp.where(slots[which] // 4 == 0, RATES[0], RATES[1]).astype(F32)

        def angles(n):
            q = n % 8 * 2 + n // 8 if which == 0 else (y_lo + n // 8) % 2 * 8 + n % 8
            rows = pl.ds(pl.multiple_of(q * OWN, 8), OWN)
            if which == 0:
                delays = dbuf_s[rows]
            else:
                odd = lax.broadcasted_iota(jnp.int32, (OWN, 128), 1) // 32 % 2
                pairs = [[dbuf_r[rows, 256 * t + 128 * a : 256 * t + 128 * a + 128] for a in range(2)] for t in range(2)]
                delays = jnp.concatenate(
                    [jnp.where(odd == halves[1], a, pltpu.roll(b, 32 + 64 * halves[1], 1)) for a, b in pairs], axis=1
                )
            turns = delays.astype(F32) * rate
            return turns - jnp.round(turns)

        def step(m, carry):
            x = jnp.concatenate([angles(2 * m), angles(2 * m + 1)], axis=0)
            z = x * x
            at = pl.ds(pl.multiple_of(m * 2 * OWN, 2 * OWN), 2 * OWN)
            tab[at, :HALF] = horner(COS, z).astype(BF16)
            tab[at, HALF:] = (horner(SIN, z) * x).astype(BF16)
            return carry

        lax.fori_loop(0, SIDE // 2, step, 0)
        for h in range(2):
            for b in range(SIDE * OWN // 128):
                value = tab[128 * b : 128 * b + 128, HALF * h : HALF * h + HALF].T
                if which == 0:
                    turned_s[HALF * h : HALF * h + HALF, 128 * b : 128 * b + 128] = value
                else:
                    turned_r[:, SIDE * OWN * h + 128 * b : SIDE * OWN * h + 128 * b + 128] = value

    def columns(rows):
        return jnp.concatenate([rows, jnp.zeros((128 - rows.shape[0], 128), F32)], axis=0).T

    steer(0)
    arrived(pw.at[:, row], 2 * SIDE - 1, PW)
    plane_sum = jnp.sum(pw[...], axis=0)
    there = pw[(1 - y_lo) * SIDE + c, :1]
    first = lax.broadcasted_iota(jnp.int32, (8, 128), 0) == 0
    for f in range(2):
        both = jnp.where(lane < OWN, power[f], there if f else pltpu.roll(there, OWN, 1))
        lv_send[f] = jnp.where(first, both, plane_sum)
    for _, p, slot, dy, _ in others[1]:
        if not dy:
            copy(lv_send.at[lax.div(slot, 4), row], lv.at[z, row], LV, peer(1, p)).start()
    lv[z] = lv_send[z // 4]

    arrived(xr.at[1, :, used], 3, X_FAR)
    for d in (4, 3, 5):
        copy(xr.at[1, zs[d], used], xr.at[1, 8 + zs[d], used], X_HAND, (across, c)).start()
    arrived(xr.at[0, :, used], 7, X_ROW)
    half = xr.at[0, pl.ds(core * 8, 8), used]
    copy(half, half, X_CORE, peer(0, c + 1 - 2 * core)).start()
    here = pw[pl.ds(y_lo * SIDE, SIDE), 0, :]
    powers[...] = columns(jnp.where(y_hi == 0, here, pltpu.roll(here, 128 - OWN, 1)))[:OWN]
    steer(1)

    low_x = lax.broadcasted_iota(jnp.int32, (OWN, 128), 1) < 64

    def unpack(axis):
        def step(n, carry):
            value = xr[axis, n, :OWN].astype(F32)
            xf[axis, pl.ds(pl.multiple_of(n * OWN, 8), OWN)] = value
            if axis == 1:
                value = pltpu.roll(value, 64, 1)
                xf[2, pl.ds(pl.multiple_of(n * OWN, 8), OWN)] = jnp.where(low_x, -value, value)
            return carry

        lax.fori_loop(0, SIDE, step, 0)

    arrived(xr.at[0, :, used], 8, X_CORE)
    unpack(0)
    arrived(xr.at[1, :, used], 9, X_COL)
    arrived(xr.at[1, :, used], 3, X_HAND)
    unpack(1)
    arrived(lv.at[:, row], 7, LV)
    marks = 0.5 * jnp.sum(lv[...], axis=0)
    level = [jnp.where(slots[which] // 4 == 0, marks[1:2], marks[2:3]) for which in range(2)]

    gain = lax.rsqrt(powers[...] + level[0])
    scaled = [
        xf[0, OWN * n : OWN * n + OWN] * gain[:, n % 8 * 2 + n // 8 : n % 8 * 2 + n // 8 + 1] for n in range(SIDE)
    ]
    both = jnp.dot(turned_s[...], jnp.concatenate(scaled, axis=0).astype(BF16), preferred_element_type=F32)
    low = lax.broadcasted_iota(jnp.int32, (HALF, 128), 1) < 64
    swapped = pltpu.roll(both[HALF:], 64, 1)
    value = (both[:HALF] + jnp.where(low, -swapped, swapped)).astype(BF16)
    for j in range(8):
        sums_s[j] = value[BEAMS * j : BEAMS * j + BEAMS]
    for d in RINGS[0][:-1]:
        copy(sums_s.at[zs[d]], part.at[0, r], SUM_U, peer(1, (1 - core) * 8 + zs[d])).start()

    gain = lax.rsqrt(columns(lv[:, 0, :])[: 2 * OWN] + level[1])
    scaled = []
    for side in (1, 2):
        for n in range(SIDE):
            own = gain[n // 8 * OWN : n // 8 * OWN + OWN, n % 8 : n % 8 + 1]
            scaled.append(xf[side, OWN * n : OWN * n + OWN] * own)
    value = jnp.dot(
        turned_r[...], jnp.concatenate(scaled, axis=0).astype(BF16), preferred_element_type=F32
    ).astype(BF16)
    for j in range(8):
        sums_r[j] = value[BEAMS * j : BEAMS * j + BEAMS]
    for dx, dy in ((dx, dy) for dx in RINGS[1] for dy in (1, 0)):
        y, xx, h = flip(y_hi, dy), lax.div(xs[dx], 2), halves[1]
        a = lax.div(xx, 2)
        j = 4 * y + 2 * lax.rem(xx, 2) + a + h - 2 * a * h
        copy(sums_r.at[j], part.at[1, c], SUM_V, (across, y * 8 + xs[dx] + h)).start()

    @pl.when(jnp.logical_not(holder[0]))
    def _():
        copy(sums_s.at[z], part.at[0, r], SUM_U, peer(1, across)).start()

    @pl.when(holder[0])
    def _():
        part[0, r] = sums_s[z]

    def total(which):
        value = jnp.sum(part[which].astype(F32), axis=0).astype(BF16)
        block[which] = value
        return value

    @pl.when(holder[1])
    def _():
        arrived(part.at[1], SIDE, SUM_V)
        value = total(1)
        for _, p, *_ in others[1]:
            copy(block.at[1], gathered.at[1, z], ALL_V, peer(1, p)).start()
        gathered[1, z] = value

    @pl.when(holder[0])
    def _():
        arrived(part.at[0], SIDE - 1, SUM_U)
        total(0)
        for _, p in facing:
            copy(block.at[0], gathered.at[0, slots[0]], ALL_U, (across, p)).start()

    arrived(gathered.at[0], 8, ALL_U)
    low = lax.broadcasted_iota(jnp.int32, (BEAMS, 128), 1) < 64
    for k in range(8):
        u = gathered[0, k].astype(F32)
        swapped = pltpu.roll(u, 64, 1)
        swapped = jnp.where(low, swapped, -swapped)
        right[k // 4, 128 * (k % 4) : 128 * (k % 4) + 128] = jnp.concatenate(
            [u, swapped, jnp.zeros((64, 128), F32)], axis=0
        ).T.astype(BF16)
    left(pw.at[:, row], 2 * SIDE - 1, PW)
    left(xr.at[0, :, used], 7, X_ROW)
    left(xr.at[0, :, used], 8, X_CORE)
    left(xr.at[1, :, used], 9, X_COL)
    left(xr.at[1, :, used], 3, X_FAR)
    left(xr.at[1, :, used], 3, X_HAND)
    left(lv.at[:, row], 7, LV)
    left(part.at[1], 8, SUM_V)

    @pl.when(holder[0])
    def _():
        left(part.at[0], 7, SUM_U)
        left(part.at[0], SIDE, ALL_U)
        arrived(gathered.at[1], 8, ALL_V)

    @pl.when(holder[1])
    def _():
        left(part.at[0], 8, SUM_U)
        left(part.at[1], SIDE - 1, ALL_V)
        arrived(gathered.at[1], 7, ALL_V)

    for f in range(2):
        v = jnp.concatenate([gathered[1, 4 * f + k] for k in range(4)], axis=1)
        value = jnp.dot(v, right[f], preferred_element_type=F32) * (math.sqrt(WINDOWS) / STATIONS)
        out[f, 0] = value[:, :BEAMS]
        out[f, 1] = value[:, BEAMS : 2 * BEAMS]


def body(spectra, delays_s, delays_r, wl_index):
    return pl.pallas_call(
        kernel,
        out_shape=pltpu.VMEM((2, 2, BEAMS, BEAMS), F32),
        in_specs=[pl.BlockSpec(memory_space=pl.ANY)] * 3 + [pl.BlockSpec(memory_space=pltpu.SMEM)],
        out_specs=pl.BlockSpec(memory_space=pltpu.VMEM),
        scratch_shapes=[
            pltpu.VMEM((2, 2, OWN, WINDOWS), BF16),
            pltpu.VMEM((SIDE * OWN, HALF), jnp.int32),
            pltpu.VMEM((SIDE * OWN, 2 * HALF), jnp.int32),
            pltpu.VMEM((SIDE * OWN, 2 * HALF), BF16),
            pltpu.VMEM((2 * HALF, SIDE * OWN), BF16),
            pltpu.VMEM((HALF, 2 * SIDE * OWN), BF16),
            pltpu.VMEM((8, SLOT, 128), BF16),
            pltpu.VMEM((2, SIDE, SLOT, 128), BF16),
            pltpu.VMEM((3, SIDE * OWN, 128), F32),
            pltpu.VMEM((8, 128), F32),
            pltpu.VMEM((2 * SIDE, 8, 128), F32),
            pltpu.VMEM((OWN, 128), F32),
            pltpu.VMEM((2, 8, 128), F32),
            pltpu.VMEM((8, 8, 128), F32),
            pltpu.VMEM((8, BEAMS, 128), BF16),
            pltpu.VMEM((8, BEAMS, 128), BF16),
            pltpu.VMEM((2, SIDE, BEAMS, 128), BF16),
            pltpu.VMEM((2, BEAMS, 128), BF16),
            pltpu.VMEM((2, 8, BEAMS, 128), BF16),
            pltpu.VMEM((2, 512, 128), BF16),
            pltpu.SemaphoreType.DMA((3,)),
            pltpu.SemaphoreType.DMA((11,)),
            pltpu.SemaphoreType.DMA((11,)),
        ],
        compiler_params=pltpu.CompilerParams(collective_id=0, has_side_effects=True),
    )(spectra, delays_s, delays_r, wl_index)


def solution(mesh):
    in_specs = (P(None, None, ("row", "col"), None), P("row", None), P("col", None), P())
    out_specs = P(None, None, "col", "row")
    return jax.shard_map(body, mesh=mesh, in_specs=in_specs, out_specs=out_specs, check_vma=False)
```

time: 32.7 us -> 32.3 us (0.988)
  Pallas kernels: 32 us -> 31.5 us
    pallas_call x1, Pallas kernels: 32 us -> 31.5 us  [body(): pl.pallas_call(kernel, out_shape=pltpu.VMEM((2, 2, BEAMS, BEAMS), F32), i...]
where the time goes in v3:
time: 32.3 us; the launch traced here: 32.2 us
  Pallas kernels  31.5 us (98%)
  local copies, waits for them, and re-layouts  0.63 us (2%)
    pallas_call x1, Pallas kernels, body(): pl.pallas_call(kernel, out_shape=pltpu.VMEM((2, 2, BEAMS, BEAMS), F32), i...  31.5 us

profile of v3, /device:TPU:1, one launch (start us, length us, event | category | flops | bytes accessed | tf_op | source)
XLA Modules:
  0.0 32.2 jit_solution(606055515165902761)
XLA Ops:
  0.0 31.5 %shard_map.46 = f32[2,2,32,32]{3,2,1,0:T(8,128)S(1)} custom-call(bf16[2,2,40,256]{3,2,1,0:T(8,128)(2,1)} %spec_hbm.1, s32[640,512]{1,0:T(8,128)} %ds_hbm.1, s32[640,512]{1,0:T(8,128)} %dr_hbm.1, s32[2]{0:T(128)} %wl.1), custom_call_target="tpu_custom_call" | custom-call | tf_op jit(solution)/shard_map/pallas_call | solution.py:323
  31.5 0.6 %copy.6 = f32[2,2,32,32]{3,2,1,0:T(8,128)} copy(f32[2,2,32,32]{3,2,1,0:T(8,128)S(1)} %shard_map.46) | data formatting | bytes 32768

commit v4 on v3

--- a/solution.py
+++ b/solution.py
@@ -132,7 +132,7 @@
             for k, value in ((2 * t, first), (2 * t + 1, second)):
                 pk[4 * f + k] = jnp.concatenate([value, jnp.zeros((SLOT - OWN, 128), F32)], axis=0).astype(BF16)
     used = pl.ds(0, OWN)
-    for _, p, slot, dy, far in others[1]:
+    for _, p, slot, dy, far in sorted(others[1], key=lambda item: not item[4]):
         if not (far and dy):
             copy(pk.at[slot, used], xr.at[1, 8 * dy + z, used], X_FAR if far else X_COL, peer(1, p)).start()
     xr[1, z] = pk[slots[1]]
@@ -204,8 +204,9 @@
 
     low_x = lax.broadcasted_iota(jnp.int32, (OWN, 128), 1) < 64
 
-    def unpack(axis):
-        def step(n, carry):
+    def unpack(axis, start, stop):
+        def step(i, carry):
+            n = i if axis == 0 else i // 8 * 8 + (z + 6 + i) % 8
             value = xr[axis, n, :OWN].astype(F32)
             xf[axis, pl.ds(pl.multiple_of(n * OWN, 8), OWN)] = value
             if axis == 1:
@@ -213,13 +214,14 @@
                 xf[2, pl.ds(pl.multiple_of(n * OWN, 8), OWN)] = jnp.where(low_x, -value, value)
             return carry
 
-        lax.fori_loop(0, SIDE, step, 0)
+        lax.fori_loop(start, stop, step, 0)
 
     arrived(xr.at[0, :, used], 8, X_CORE)
-    unpack(0)
+    unpack(0, 0, SIDE)
     arrived(xr.at[1, :, used], 9, X_COL)
+    unpack(1, 0, SIDE - 3)
     arrived(xr.at[1, :, used], 3, X_HAND)
-    unpack(1)
+    unpack(1, SIDE - 3, SIDE)
     arrived(lv.at[:, row], 7, LV)
     marks = 0.5 * jnp.sum(lv[...], axis=0)
     level = [jnp.where(slots[which] // 4 == 0, marks[1:2], marks[2:3]) for which in range(2)]

time: 32.3 us -> 31.9 us (0.988)
  Pallas kernels: 31.5 us -> 31.1 us
    pallas_call x1, Pallas kernels: 31.5 us -> 31.1 us  [body(): pl.pallas_call(kernel, out_shape=pltpu.VMEM((2, 2, BEAMS, BEAMS), F32), i...]
where the time goes in v4:
time: 31.9 us; the launch traced here: 31.8 us
  Pallas kernels  31.1 us (97%)
  local copies, waits for them, and re-layouts  0.63 us (2%)
    pallas_call x1, Pallas kernels, body(): pl.pallas_call(kernel, out_shape=pltpu.VMEM((2, 2, BEAMS, BEAMS), F32), i...  31.1 us

profile of v4, /device:TPU:1, one launch (start us, length us, event | category | flops | bytes accessed | tf_op | source)
XLA Modules:
  0.0 31.8 jit_solution(12258147733933302752)
XLA Ops:
  0.0 31.1 %shard_map.46 = f32[2,2,32,32]{3,2,1,0:T(8,128)S(1)} custom-call(bf16[2,2,40,256]{3,2,1,0:T(8,128)(2,1)} %spec_hbm.1, s32[640,512]{1,0:T(8,128)} %ds_hbm.1, s32[640,512]{1,0:T(8,128)} %dr_hbm.1, s32[2]{0:T(128)} %wl.1), custom_call_target="tpu_custom_call" | custom-call | tf_op jit(solution)/shard_map/pallas_call | solution.py:325
  31.1 0.6 %copy.6 = f32[2,2,32,32]{3,2,1,0:T(8,128)} copy(f32[2,2,32,32]{3,2,1,0:T(8,128)S(1)} %shard_map.46) | data formatting | bytes 32768

commit v5 on v4

--- a/solution.py
+++ b/solution.py
@@ -132,14 +132,14 @@
             for k, value in ((2 * t, first), (2 * t + 1, second)):
                 pk[4 * f + k] = jnp.concatenate([value, jnp.zeros((SLOT - OWN, 128), F32)], axis=0).astype(BF16)
     used = pl.ds(0, OWN)
+    for _, p, slot, cross, _ in others[0]:
+        if not cross:
+            copy(pk.at[slot, used], xr.at[0, core * 8 + c // 2, used], X_ROW, peer(0, p)).start()
+    xr[0, core * 8 + c // 2] = pk[slots[0]]
     for _, p, slot, dy, far in sorted(others[1], key=lambda item: not item[4]):
         if not (far and dy):
             copy(pk.at[slot, used], xr.at[1, 8 * dy + z, used], X_FAR if far else X_COL, peer(1, p)).start()
     xr[1, z] = pk[slots[1]]
-    for _, p, slot, cross, _ in others[0]:
-        if not cross:
-            copy(pk.at[slot, used], xr.at[0, core * 8 + c // 2, used], X_ROW, peer(0, p)).start()
-    xr[0, core * 8 + c // 2] = pk[slots[0]]
 
     def steer(which):
         loads[which].wait()
@@ -316,9 +316,9 @@
 
     for f in range(2):
         v = jnp.concatenate([gathered[1, 4 * f + k] for k in range(4)], axis=1)
-        value = jnp.dot(v, right[f], preferred_element_type=F32) * (math.sqrt(WINDOWS) / STATIONS)
+        value = jnp.dot(v, right[f, :, : 2 * BEAMS], preferred_element_type=F32) * (math.sqrt(WINDOWS) / STATIONS)
         out[f, 0] = value[:, :BEAMS]
-        out[f, 1] = value[:, BEAMS : 2 * BEAMS]
+        out[f, 1] = value[:, BEAMS:]
 
 
 def body(spectra, delays_s, delays_r, wl_index):

time: 31.9 us -> 31.8 us (level)
  no operation moved by 1% of the time
where the time goes in v5:
time: 31.8 us; the launch traced here: 31.7 us
  Pallas kernels  31.1 us (98%)
  local copies, waits for them, and re-layouts  0.63 us (2%)
    pallas_call x1, Pallas kernels, body(): pl.pallas_call(kernel, out_shape=pltpu.VMEM((2, 2, BEAMS, BEAMS), F32), i...  31.1 us

profile of v5, /device:TPU:1, one launch (start us, length us, event | category | flops | bytes accessed | tf_op | source)
XLA Modules:
  0.0 31.7 jit_solution(14419953322181286147)
XLA Ops:
  0.0 31.1 %shard_map.46 = f32[2,2,32,32]{3,2,1,0:T(8,128)S(1)} custom-call(bf16[2,2,40,256]{3,2,1,0:T(8,128)(2,1)} %spec_hbm.1, s32[640,512]{1,0:T(8,128)} %ds_hbm.1, s32[640,512]{1,0:T(8,128)} %dr_hbm.1, s32[2]{0:T(128)} %wl.1), custom_call_target="tpu_custom_call" | custom-call | tf_op jit(solution)/shard_map/pallas_call | solution.py:325
  31.1 0.6 %copy.6 = f32[2,2,32,32]{3,2,1,0:T(8,128)} copy(f32[2,2,32,32]{3,2,1,0:T(8,128)S(1)} %shard_map.46) | data formatting | bytes 32768

commit v6 on v5

--- a/solution.py
+++ b/solution.py
@@ -88,16 +88,16 @@
     ]
     load_x = pltpu.make_async_copy(spec_hbm, xin, load.at[2])
     load_x.start()
-    for item in loads:
-        item.start()
     row = pl.ds(0, MESSAGE)
     barrier = pltpu.get_barrier_semaphore()
     plane = [(hop, (r, p)) for hop, p, *_ in others[0]] + [(hop, (across, p)) for hop, p in facing]
     column = [(hop, (p, c)) for hop, p, slot, dy, far in others[1] if not (dy and (far or hop == 1))]
     farthest = lambda devices: [device for _, device in sorted(devices, key=lambda item: -item[0])]
-    greeted = farthest(plane + column)
+    greeted = farthest(column + plane)
     for device in greeted:
         pl.semaphore_signal(barrier, inc=1, device_id=device, device_id_type=MESH)
+    for item in loads:
+        item.start()
 
     pw_send[...] = jnp.zeros((8, 128), F32)
     load_x.wait()

time: 31.8 us -> 31.9 us (level)
  no operation moved by 1% of the time
where the time goes in v6:
time: 31.9 us; the launch traced here: 31.7 us
  Pallas kernels  31.1 us (97%)
  local copies, waits for them, and re-layouts  0.63 us (2%)
    pallas_call x1, Pallas kernels, body(): pl.pallas_call(kernel, out_shape=pltpu.VMEM((2, 2, BEAMS, BEAMS), F32), i...  31.1 us

profile of v6, /device:TPU:1, one launch (start us, length us, event | category | flops | bytes accessed | tf_op | source)
XLA Modules:
  0.0 31.7 jit_solution(5455455948534990136)
XLA Ops:
  0.0 31.1 %shard_map.46 = f32[2,2,32,32]{3,2,1,0:T(8,128)S(1)} custom-call(bf16[2,2,40,256]{3,2,1,0:T(8,128)(2,1)} %spec_hbm.1, s32[640,512]{1,0:T(8,128)} %ds_hbm.1, s32[640,512]{1,0:T(8,128)} %dr_hbm.1, s32[2]{0:T(128)} %wl.1), custom_call_target="tpu_custom_call" | custom-call | tf_op jit(solution)/shard_map/pallas_call | solution.py:325
  31.1 0.6 %copy.6 = f32[2,2,32,32]{3,2,1,0:T(8,128)} copy(f32[2,2,32,32]{3,2,1,0:T(8,128)S(1)} %shard_map.46) | data formatting | bytes 32768
